TPU v7x, 128 devices: a whole 4x4x4 slice. The times are simulated.
128 devices in a mesh: client: 16 (over y_lo, x, core), unit: 8 (over z, y_hi).
Axes of the slice: x: 4, y: 4 (y_hi: 2, y_lo: 2; y = y_hi * 2 + y_lo), z: 4, core: 2. Of those that a mesh axis runs over, the one named last changes fastest.
Arguments:
- token_ids: int32 [256], replicated, may hold values from 0 to 65535
- embed_table: bfloat16 [65536, 4096], P(('client', 'unit')), may hold values from -6 to 6
- norm_gain: float32 [4096], replicated, may hold values from 0.5 to 1.5
- client_gate: bfloat16 [16, 4096, 7168], P('client', None, 'unit'), may hold values from -0.09375 to 0.09375
- client_up: bfloat16 [16, 4096, 7168], P('client', None, 'unit'), may hold values from -0.09375 to 0.09375
- ref_gate: bfloat16 [4096, 7168], P('client', 'unit'), may hold values from -0.09375 to 0.09375
- ref_up: bfloat16 [4096, 7168], P('client', 'unit'), may hold values from -0.09375 to 0.09375
Outputs:
- merged: float32 [7168, 256], P('unit')
- score: float32 [16, 7168], P('client', 'unit')
All inputs are finite; a program needn't handle non-finite values.
Results may differ from a plain program's by a relative error of at most 0.014.
Values may be sent and summed in bfloat16 or wider, within the bound.
A program may use at most 128 MiB of HBM per device.

v0:
```python
import jax
import jax.numpy as jnp
from jax import lax
from jax.sharding import PartitionSpec as P

sharpness = 40.0
block_cols = 2048


def split_up(shard, dim, count):
    before, after = (shard.shape[:dim], shard.shape[dim + 1 :])
    return jnp.moveaxis(shard.reshape(*before, count, -1, *after), dim, 0)


def summed_on_arrival(shard, axis, dim):
    count = lax.axis_size(axis)
    blocks = lax.all_to_all(split_up(shard, dim, count), axis, 0, 0, tiled=True)
    return jnp.sum(blocks, axis=0)


def sent_together(arrays, axis, dim, along):
    widths = [a.shape[along] for a in arrays]
    both = jnp.concatenate(arrays, axis=along)
    result = summed_on_arrival(both, axis, dim)
    return tuple(jnp.split(result, [sum(widths[:k]) for k in range(1, len(widths))], axis=along))


def laid_out(blocks, dim):
    dims = list(blocks.shape[1:])
    dims[dim] *= blocks.shape[0]
    return jnp.moveaxis(blocks, 0, dim).reshape(dims)


def copy_for_each(shard, axis):
    copies = jnp.broadcast_to(shard, (lax.axis_size(axis), *shard.shape))
    return lax.all_to_all(copies, axis, split_axis=0, concat_axis=0, tiled=True)


def gather_directly(shard, axis, dim):
    return laid_out(copy_for_each(shard, axis), dim)


def filled_up(lines, count):
    spare = -len(lines) % count
    return jnp.pad(lines, [(0, spare)] + [(0, 0)] * (lines.ndim - 1))


def sent_and_summed(shard, axis, dim):
    blocks = split_up(shard, dim, lax.axis_size(axis))
    arrived = lax.all_to_all(blocks, axis, split_axis=0, concat_axis=0, tiled=True)
    return arrived.astype(jnp.float32).sum(axis=0)


def nested_sum(shard, axes):
    lines = shard.reshape(-1, shard.shape[-1])
    padded = filled_up(lines, lax.axis_size(axes))
    whole = gather_directly(sent_and_summed(padded, axes, 0).astype(jnp.bfloat16), axes, 0)
    return lax.slice_in_dim(whole, 0, len(lines)).reshape(shard.shape).astype(jnp.float32)


def standardize(hidden):
    center = jnp.mean(hidden, axis=0, keepdims=True)
    shifted = hidden - center
    spread = jnp.sqrt(jnp.mean(shifted * shifted, axis=0, keepdims=True) + 1e-06)
    return (shifted / spread).astype(jnp.bfloat16)


def block_ranges(length):
    return [(offset, min(block_cols, length - offset)) for offset in range(0, length, block_cols)]


def rms_scaled(values, norm_gain):
    scale = lax.rsqrt(jnp.mean(values * values, axis=1, keepdims=True) + 1e-05)
    return (values * scale * norm_gain[None, :]).astype(jnp.bfloat16)


def body(token_ids, embed_table, norm_gain, client_gate, client_up, ref_gate, ref_up):
    rows_here = embed_table.shape[0]
    table_start = (
        lax.axis_index("client") * lax.axis_size("unit") + lax.axis_index("unit")
    ) * rows_here
    table_rows = table_start + jnp.arange(rows_here, dtype=jnp.int32)
    selector = (token_ids[:, None] == table_rows[None, :]).astype(jnp.bfloat16)
    partial_rows = jnp.dot(selector, embed_table, preferred_element_type=jnp.float32)
    embedded = lax.psum(partial_rows, ("client", "unit"))
    normed = rms_scaled(embedded, norm_gain)
    token_count = normed.shape[0]
    inverse_tokens = 1.0 / token_count
    gate_local = jnp.dot(normed, client_gate[0], preferred_element_type=jnp.float32)
    up_local = jnp.dot(normed, client_up[0], preferred_element_type=jnp.float32)
    client_std = standardize(jax.nn.silu(gate_local) * up_local)
    row_span = ref_gate.shape[0]
    normed_slice = lax.dynamic_slice_in_dim(
        normed, lax.axis_index("client") * row_span, row_span, 1
    )
    gate_part = jnp.dot(normed_slice, ref_gate, preferred_element_type=jnp.float32)
    up_part = jnp.dot(normed_slice, ref_up, preferred_element_type=jnp.float32)
    gate_share, up_share = sent_together((gate_part, up_part), "client", 1, 0)
    ref_piece = standardize(jax.nn.silu(gate_share) * up_share)
    ref_std = gather_directly(ref_piece, "client", 1)
    local_units = client_std.shape[1]
    segment = lax.all_gather(client_std, "unit", axis=1, tiled=True)
    numerator = jnp.zeros((local_units, token_count), jnp.float32)
    colsum = jnp.zeros((local_units,), jnp.float32)
    weighted = jnp.zeros((local_units,), jnp.float32)
    for offset, width in block_ranges(segment.shape[1]):
        columns = segment[:, offset : offset + width]
        correlation = (
            jnp.dot(columns.T, ref_std, preferred_element_type=jnp.float32) * inverse_tokens
        )
        weights = jnp.exp(sharpness * correlation)
        numerator = numerator + lax.dot_general(
            weights.astype(jnp.bfloat16),
            columns,
            (((0,), (1,)), ((), ())),
            preferred_element_type=jnp.float32,
        )
        colsum = colsum + jnp.sum(weights, axis=0)
        weighted = weighted + jnp.sum(weights * correlation, axis=0)
    numerator, colsum, weighted = (numerator, colsum, weighted)
    matched = numerator / colsum[:, None]
    score = (weighted / colsum)[None, :]
    merged = nested_sum(matched.astype(jnp.bfloat16), "client") / lax.axis_size("client")
    return (merged, score)


def solution(mesh):
    in_specs = (
        P(),
        P(("client", "unit"), None),
        P(),
        P("client", None, "unit"),
        P("client", None, "unit"),
        P("client", "unit"),
        P("client", "unit"),
    )
    out_specs = (P("unit", None), P("client", "unit"))
    return jax.shard_map(body, mesh=mesh, in_specs=in_specs, out_specs=out_specs, check_vma=False)
```

profile of v0, /device:TPU:1, one launch (start us, length us, event | category | flops | bytes accessed | tf_op | source)
XLA Modules:
  0.0 315.0 jit_solution(14013043354471950132)
XLA Ops:
  7.2 5.5 %fusion.51 = f32[256,4096]{1,0:T(8,128)} fusion(bf16[512,4096]{1,0:T(8,128)(2,1)} %param.8, s32[512]{0:T(512)S(1)} %iota_add_fusion, s32[256]{0:T(256)} %param.7), kind=kOutput, calls=%fused_computation.49 | convolution fusion | flops 1073872896 | bytes 8391680 | tf_op jit(solution)/shard_map/dot_general | solution.py:84
  12.8 157.7 %all-reduce.2.cloned.1.call-done = f32[256,4096]{1,0:T(8,128)} async-done(((f32[256,4096]{1,0:T(8,128)}), f32[256,4096]{1,0:T(8,128)}) %all-reduce.2.cloned.1.call-update) | async-done | bytes 4194320 | tf_op jit(solution)/shard_map/psum | solution.py:85
  170.5 2.7 multiply_reduce_fusion.3
  173.2 0.7 copy-done.2
  174.6 5.7 %fusion.2 = f32[256,896]{1,0:T(8,128)S(1)} fusion(bf16[256,4096]{1,0:T(8,128)(2,1)S(1)} %multiply_convert_fusion, bf16[1,4096,896]{2,1,0:T(8,128)(2,1)} %param.10), kind=kOutput, calls=%fused_computation.2 | convolution fusion | flops 1879048192 | bytes 10354688 | tf_op jit(solution)/shard_map/dot_general | solution.py:89
  180.3 2.4 fusion.69
  182.9 0.9 divide_convert_fusion
  184.6 1.8 copy.9
  186.3 31.7 %all_to_all.20 = f32[16,512,56]{1,2,0:T(8,128)S(1)} all-to-all(f32[16,512,56]{1,2,0:T(8,128)} %bitcast.27), channel_id=1, replica_groups=mesh['client'=16,'unit'=8] {'client'}, dimensions={0} | all-to-all | bytes 3670016 | tf_op jit(solution)/shard_map/all_to_all | solution.py:17
  218.6 13.6 %all_to_all.21 = bf16[16,256,56]{1,2,0:T(8,128)(2,1)S(1)} all-to-all(bf16[16,256,56]{1,2,0:T(8,128)(2,1)S(1)} %broadcast_in_dim.4), channel_id=1, replica_groups=mesh['client'=16,'unit'=8] {'client'}, dimensions={0} | all-to-all | bytes 917504 | tf_op jit(solution)/shard_map/all_to_all | solution.py:36
  232.2 32.9 %all-gather.2.cloned.1.call-done = bf16[256,7168]{1,0:T(8,128)(2,1)} async-done(((bf16[256,896]{1,0:T(8,128)(2,1)}), bf16[256,7168]{1,0:T(8,128)(2,1)}) %all-gather.2.cloned.1.call-update) | async-done | bytes 3670032 | tf_op jit(solution)/shard_map/all_gather | solution.py:102
  265.1 3.4 %multiply_reduce_fusion.2 = (f32[896]{0:T(1024)S(1)}, f32[896]{0:T(1024)S(1)}, f32[2048,896]{1,0:T(8,128)S(1)}) fusion(bf16[256,896]{0,1:T(8,128)(2,1)S(1)} %bitcast.29, bf16[256,7168]{1,0:T(8,128)(2,1)} %all-gather.2.cloned.1.call-done), kind=kOutput, calls=%fused_computation.6 | convolution fusion | flops 948697344 | bytes 8854528 | tf_op jit(solution)/shard_map/dot_general | solution.py:109
  268.5 2.2 multiply_reduce_fusion.1
  270.7 2.2 multiply_reduce_fusion
  272.9 1.1 multiply_reduce_fusion.4
  274.0 1.2 fusion.10
  275.2 1.2 fusion.33
  276.4 1.2 fusion.30
  277.6 0.8 fusion.39
  278.3 14.3 %all_to_all.22 = bf16[16,56,256]{2,1,0:T(8,128)(2,1)S(1)} all-to-all(bf16[16,56,256]{2,1,0:T(8,128)(2,1)S(1)} %bitcast.33), channel_id=1, replica_groups=mesh['client'=16,'unit'=8] {'client'}, dimensions={0} | all-to-all | bytes 917504 | tf_op jit(solution)/shard_map/all_to_all | solution.py:50
  292.7 0.8 broadcast_in_dim.5
  293.5 4.7 %all-to-all-start.3 = ((bf16[16,56,256]{2,1,0:T(8,128)(2,1)}), bf16[16,56,256]{2,1,0:T(8,128)(2,1)S(1)}, u32[]{:S(2)}, u32[]{:S(2)}) async-start(bf16[16,56,256]{2,1,0:T(8,128)(2,1)} %broadcast_in_dim.5), calls=%async_computation.3 | async-start | bytes 917504 | tf_op jit(solution)/shard_map/all_to_all | solution.py:36
  298.9 8.4 %all-to-all-done.3 = bf16[16,56,256]{2,1,0:T(8,128)(2,1)S(1)} async-done(((bf16[16,56,256]{2,1,0:T(8,128)(2,1)}), bf16[16,56,256]{2,1,0:T(8,128)(2,1)S(1)}, u32[]{:S(2)}, u32[]{:S(2)}) %all-to-all-start.3) | async-done | bytes 458784 | tf_op jit(solution)/shard_map/all_to_all | solution.py:36
  307.2 1.0 convert_multiply_fusion
  (39 shorter events, 2.8 us)
Async XLA Ops:
  7.2 176.6 %copy-start = (bf16[256,896]{1,0:T(8,128)(2,1)S(1)}, bf16[256,896]{1,0:T(8,128)(2,1)}, u32[]{:S(2)}) copy-start(bf16[256,896]{1,0:T(8,128)(2,1)} %param.13) | copy-start | bytes 1376260
  7.2 163.3 %all-reduce.2.cloned.1.call-start = ((), (), s32[]{:S(2)}) async-start(), calls=%async_computation.4 | async-start | bytes 8388608 | tf_op jit(solution)/shard_map/psum | solution.py:85
  12.8 160.5 %copy-start.5 = (f32[4096]{0:T(1024)S(1)}, f32[4096]{0:T(1024)}, u32[]{:S(2)}) copy-start(f32[4096]{0:T(1024)} %param.9) | copy-start | bytes 49156
  12.8 252.3 %all-gather.2.cloned.1.call-start = ((), (), s32[]{:S(2)}) async-start(), calls=%async_computation.5 | async-start | bytes 4128768 | tf_op jit(solution)/shard_map/all_gather | solution.py:102
  170.5 3.4 %copy-start.2 = (f32[256,4096]{1,0:T(8,128)S(1)}, f32[256,4096]{1,0:T(8,128)}, u32[]{:S(2)}) copy-start(f32[256,4096]{1,0:T(8,128)} %all-reduce.2.cloned.1.call-done) | copy-start | bytes 12582916
  174.0 6.3 %slice-start = ((s8[7340032]{0:T(1024)(128)(4,1)}), s8[3145728]{0:T(1024)(128)(4,1)S(1)}, s32[]{:S(2)}) async-start(s8[7340032]{0:T(1024)(128)(4,1)} %bitcast.34), calls=%async_computation.6 | async-start | bytes 6291456
  174.5 5.7 %slice-start.1 = ((s8[7340032]{0:T(1024)(128)(4,1)}), s8[4194304]{0:T(1024)(128)(4,1)S(1)}, s32[]{:S(2)}) async-start(s8[7340032]{0:T(1024)(128)(4,1)} %bitcast.34), calls=%async_computation.7 | async-start | bytes 8388608
  182.8 1.4 copy-start.4
  265.1 3.4 %copy-start.3 = (bf16[256,7168]{1,0:T(8,128)(2,1)S(1)}, bf16[256,7168]{1,0:T(8,128)(2,1)}, u32[]{:S(2)}) copy-start(bf16[256,7168]{1,0:T(8,128)(2,1)} %all-gather.2.cloned.1.call-done) | copy-start | bytes 11010052
  277.5 30.6 %copy-start.1 = (bf16[256,896]{1,0:T(8,128)(2,1)S(1)}, bf16[256,896]{1,0:T(8,128)(2,1)}, u32[]{:S(2)}) copy-start(bf16[256,896]{1,0:T(8,128)(2,1)} %param.13) | copy-start | bytes 1376260
  293.5 13.7 %all-to-all-start.3 = ((bf16[16,56,256]{2,1,0:T(8,128)(2,1)}), bf16[16,56,256]{2,1,0:T(8,128)(2,1)S(1)}, u32[]{:S(2)}, u32[]{:S(2)}) async-start(bf16[16,56,256]{2,1,0:T(8,128)(2,1)} %broadcast_in_dim.5), calls=%async_computation.3 | async-start | bytes 917504 | tf_op jit(solution)/shard_map/all_to_all | solution.py:36
Sparse Core Ops, SparseCore 0:
  12.9 157.5 all-reduce.1
  183.9 81.1 all-gather.1
where the time goes:
time: 315 us
  waiting for transfers between devices  199 us (63%)
  blocking collectives  59.6 us (19%)
  matrix products  27.4 us (9%)
  between operations  14.3 us (5%)
  other arithmetic  6.02 us (2%)
  starting transfers between devices  4.82 us (2%)
  local copies, waits for them, and re-layouts  3.95 us (1%)
    psum x1, waiting for transfers between devices, body(): embedded = lax.psum(partial_rows, ('client', 'unit'))  158 us
    all_gather x1, waiting for transfers between devices, body(): segment = lax.all_gather(client_std, 'unit', axis=1, tiled=True)  32.9 us
    all_to_all x1, blocking collectives, summed_on_arrival(): blocks = lax.all_to_all(split_up(shard, dim, count), axis, 0, 0, tiled=True)  31.7 us
    all_to_all x1, blocking collectives, sent_and_summed(): lax.all_to_all(blocks, axis, split_axis=0, concat_axis=0, tiled=True)  14.3 us
    all_to_all x1, blocking collectives, copy_for_each(): return lax.all_to_all(copies, axis, split_axis=0, concat_axis=0, tiled=True)  13.6 us
    dot_general x4, matrix products, body(): jnp.dot(columns.T, ref_std, preferred_element_type=jnp.float32)  8.84 us
    all_to_all x1, waiting for transfers between devices, copy_for_each(): return lax.all_to_all(copies, axis, split_axis=0, concat_axis=0, tiled=True)  8.36 us
  transfers between devices with their start and end apart: 3, of which 3 were waited for; matrix products, arithmetic and copies ran while one was open for 1% of the time, Pallas kernels for 0%

commit v1 on v0

--- a/solution.py
+++ b/solution.py
@@ -82,7 +82,7 @@
     table_rows = table_start + jnp.arange(rows_here, dtype=jnp.int32)
     selector = (token_ids[:, None] == table_rows[None, :]).astype(jnp.bfloat16)
     partial_rows = jnp.dot(selector, embed_table, preferred_element_type=jnp.float32)
-    embedded = lax.psum(partial_rows, ("client", "unit"))
+    embedded = lax.psum(lax.psum(partial_rows, "client"), "unit")
     normed = rms_scaled(embedded, norm_gain)
     token_count = normed.shape[0]
     inverse_tokens = 1.0 / token_count

time: 315 us -> 479 us (1.52)
  waiting for transfers between devices: 199 us -> 362 us
    psum x1 -> x2, waiting for transfers between devices: 158 us -> 321 us  [body(): embedded = lax.psum(lax.psum(partial_rows, 'client'), 'unit')]
  transfers between devices with their start and end apart: 3 -> 4, of which waited for: 3 -> 4; matrix products, arithmetic and copies ran while one was open for 1% -> 1% of each run, Pallas kernels for 0% -> 0%
where the time goes in v1:
time: 479 us; the launch traced here: 478 us
  waiting for transfers between devices  362 us (76%)
  blocking collectives  60.1 us (13%)
  matrix products  27.4 us (6%)
  between operations  14 us (3%)
  other arithmetic  6.02 us (1%)
  starting transfers between devices  4.86 us (1%)
    psum x2, waiting for transfers between devices, body(): embedded = lax.psum(lax.psum(partial_rows, 'client'), 'unit')  321 us
    all_gather x1, waiting for transfers between devices, body(): segment = lax.all_gather(client_std, 'unit', axis=1, tiled=True)  32.9 us
    all_to_all x1, blocking collectives, summed_on_arrival(): blocks = lax.all_to_all(split_up(shard, dim, count), axis, 0, 0, tiled=True)  32.1 us
    all_to_all x1, blocking collectives, sent_and_summed(): lax.all_to_all(blocks, axis, split_axis=0, concat_axis=0, tiled=True)  14.3 us
    all_to_all x1, blocking collectives, copy_for_each(): return lax.all_to_all(copies, axis, split_axis=0, concat_axis=0, tiled=True)  13.7 us
  transfers between devices with their start and end apart: 4, of which 4 were waited for; matrix products, arithmetic and copies ran while one was open for 1% of the time, Pallas kernels for 0%

profile of v1, /device:TPU:1, one launch (start us, length us, event | category | flops | bytes accessed | tf_op | source)
XLA Modules:
  0.0 478.4 jit_solution(14996742242532336033)
XLA Ops:
  7.2 5.5 %fusion.51 = f32[256,4096]{1,0:T(8,128)} fusion(bf16[512,4096]{1,0:T(8,128)(2,1)} %param.8, s32[512]{0:T(512)S(1)} %iota_add_fusion, s32[256]{0:T(256)} %param.7), kind=kOutput, calls=%fused_computation.49 | convolution fusion | flops 1073872896 | bytes 8391680 | tf_op jit(solution)/shard_map/dot_general | solution.py:84
  12.8 132.0 %all-reduce.3.cloned.1.call-done = f32[256,4096]{1,0:T(8,128)} async-done(((f32[256,4096]{1,0:T(8,128)}), f32[256,4096]{1,0:T(8,128)}) %all-reduce.3.cloned.1.call-update) | async-done | bytes 4194320 | tf_op jit(solution)/shard_map/psum | solution.py:85
  145.0 188.7 %all-reduce.5.cloned.1.call-done = f32[256,4096]{1,0:T(8,128)} async-done(((f32[256,4096]{1,0:T(8,128)}), f32[256,4096]{1,0:T(8,128)}) %all-reduce.5.cloned.1.call-update) | async-done | bytes 4194320 | tf_op jit(solution)/shard_map/psum | solution.py:85
  333.6 2.7 multiply_reduce_fusion.3
  337.7 5.7 %fusion.2 = f32[256,896]{1,0:T(8,128)S(1)} fusion(bf16[256,4096]{1,0:T(8,128)(2,1)S(1)} %multiply_convert_fusion, bf16[1,4096,896]{2,1,0:T(8,128)(2,1)} %param.10), kind=kOutput, calls=%fused_computation.2 | convolution fusion | flops 1879048192 | bytes 10354688 | tf_op jit(solution)/shard_map/dot_general | solution.py:89
  343.4 2.4 fusion.69
  346.0 0.9 divide_convert_fusion
  347.7 1.8 copy.9
  349.4 32.1 %all_to_all.20 = f32[16,512,56]{1,2,0:T(8,128)S(1)} all-to-all(f32[16,512,56]{1,2,0:T(8,128)} %bitcast.27), channel_id=1, replica_groups=mesh['client'=16,'unit'=8] {'client'}, dimensions={0} | all-to-all | bytes 3670016 | tf_op jit(solution)/shard_map/all_to_all | solution.py:17
  382.2 13.7 %all_to_all.21 = bf16[16,256,56]{1,2,0:T(8,128)(2,1)S(1)} all-to-all(bf16[16,256,56]{1,2,0:T(8,128)(2,1)S(1)} %broadcast_in_dim.4), channel_id=1, replica_groups=mesh['client'=16,'unit'=8] {'client'}, dimensions={0} | all-to-all | bytes 917504 | tf_op jit(solution)/shard_map/all_to_all | solution.py:36
  395.9 32.9 %all-gather.2.cloned.1.call-done = bf16[256,7168]{1,0:T(8,128)(2,1)} async-done(((bf16[256,896]{1,0:T(8,128)(2,1)}), bf16[256,7168]{1,0:T(8,128)(2,1)}) %all-gather.2.cloned.1.call-update) | async-done | bytes 3670032 | tf_op jit(solution)/shard_map/all_gather | solution.py:102
  428.8 3.4 multiply_reduce_fusion.2
  432.2 2.2 multiply_reduce_fusion.1
  434.4 2.2 multiply_reduce_fusion
  436.6 1.1 multiply_reduce_fusion.4
  437.7 1.2 fusion.10
  438.9 1.2 fusion.33
  440.1 1.2 fusion.30
  441.2 0.8 fusion.39
  442.0 14.3 %all_to_all.22 = bf16[16,56,256]{2,1,0:T(8,128)(2,1)S(1)} all-to-all(bf16[16,56,256]{2,1,0:T(8,128)(2,1)S(1)} %bitcast.33), channel_id=1, replica_groups=mesh['client'=16,'unit'=8] {'client'}, dimensions={0} | all-to-all | bytes 917504 | tf_op jit(solution)/shard_map/all_to_all | solution.py:50
  456.4 0.8 broadcast_in_dim.5
  457.2 4.7 all-to-all-start.3
  462.5 8.4 %all-to-all-done.3 = bf16[16,56,256]{2,1,0:T(8,128)(2,1)S(1)} async-done(((bf16[16,56,256]{2,1,0:T(8,128)(2,1)}), bf16[16,56,256]{2,1,0:T(8,128)(2,1)S(1)}, u32[]{:S(2)}, u32[]{:S(2)}) %all-to-all-start.3) | async-done | bytes 458784 | tf_op jit(solution)/shard_map/all_to_all | solution.py:36
  470.9 1.0 convert_multiply_fusion
  (42 shorter events, 3.6 us)
Async XLA Ops:
  7.2 339.8 %copy-start = (bf16[256,896]{1,0:T(8,128)(2,1)S(1)}, bf16[256,896]{1,0:T(8,128)(2,1)}, u32[]{:S(2)}) copy-start(bf16[256,896]{1,0:T(8,128)(2,1)} %param.13) | copy-start | bytes 1376260
  7.2 137.7 %all-reduce.3.cloned.1.call-start = ((), (), s32[]{:S(2)}) async-start(), calls=%async_computation.4 | async-start | bytes 8388608 | tf_op jit(solution)/shard_map/psum | solution.py:85
  12.8 320.8 %all-reduce.5.cloned.1.call-start = ((), (), s32[]{:S(2)}) async-start(), calls=%async_computation.5 | async-start | bytes 8388608 | tf_op jit(solution)/shard_map/psum | solution.py:85
  144.9 191.5 %copy-start.5 = (f32[4096]{0:T(1024)S(1)}, f32[4096]{0:T(1024)}, u32[]{:S(2)}) copy-start(f32[4096]{0:T(1024)} %param.9) | copy-start | bytes 49156
  144.9 283.9 %all-gather.2.cloned.1.call-start = ((), (), s32[]{:S(2)}) async-start(), calls=%async_computation.6 | async-start | bytes 4128768 | tf_op jit(solution)/shard_map/all_gather | solution.py:102
  333.6 3.4 copy-start.2
  337.1 6.3 %slice-start = ((s8[7340032]{0:T(1024)(128)(4,1)}), s8[3145728]{0:T(1024)(128)(4,1)S(1)}, s32[]{:S(2)}) async-start(s8[7340032]{0:T(1024)(128)(4,1)} %bitcast.34), calls=%async_computation.7 | async-start | bytes 6291456
  337.7 5.7 %slice-start.1 = ((s8[7340032]{0:T(1024)(128)(4,1)}), s8[4194304]{0:T(1024)(128)(4,1)S(1)}, s32[]{:S(2)}) async-start(s8[7340032]{0:T(1024)(128)(4,1)} %bitcast.34), calls=%async_computation.8 | async-start | bytes 8388608
  345.9 1.4 copy-start.4
  428.8 3.4 copy-start.3
  441.2 30.6 %copy-start.1 = (bf16[256,896]{1,0:T(8,128)(2,1)S(1)}, bf16[256,896]{1,0:T(8,128)(2,1)}, u32[]{:S(2)}) copy-start(bf16[256,896]{1,0:T(8,128)(2,1)} %param.13) | copy-start | bytes 1376260
  457.2 13.7 %all-to-all-start.3 = ((bf16[16,56,256]{2,1,0:T(8,128)(2,1)}), bf16[16,56,256]{2,1,0:T(8,128)(2,1)S(1)}, u32[]{:S(2)}, u32[]{:S(2)}) async-start(bf16[16,56,256]{2,1,0:T(8,128)(2,1)} %broadcast_in_dim.5), calls=%async_computation.3 | async-start | bytes 917504 | tf_op jit(solution)/shard_map/all_to_all | solution.py:36
Sparse Core Ops, SparseCore 0:
  12.9 131.9 all-reduce.2
  147.4 186.1 all-reduce.4
  347.0 81.7 all-gather.1
